TPU v7x, 32 devices: a whole 2x2x4 slice. The times are simulated.
32 devices in a mesh: dp: 8 (over z, x), feat: 4 (over y, core).
Axes of the slice: x: 2, y: 2, z: 4, core: 2. Of those that a mesh axis runs over, the one named last changes fastest.
Arguments:
- member_feats: bfloat16 [32768, 256], P(('dp', 'feat')), may hold values from -6 to 6
- labels: int32 [32768], P(('dp', 'feat')), may hold values 0 or 1
- fixed_values: bfloat16 [32768, 2048], P('dp', 'feat'), may hold values from -6 to 6
- fixed_blocks: int32 [32768, 4], P('dp', 'feat'), may hold values from 0 to 511
- fixed_coef: float32 [2048, 512], P('feat'), may hold values from -0.12 to 0.12
- member_coef: float32 [128, 256], P(('dp', 'feat')), may hold values from -0.36 to 0.36
- row_slot: int32 [32768], P(('dp', 'feat')), may hold values from 0 to 2047, as said below
- tile_source: int32 [77824], P(('dp', 'feat')), may hold values from 0 to 2048, as said below
- member_tiles: int32 [128], P(('dp', 'feat')), may hold values from 1 to 16, as said below
Outputs:
- margin: float32 [32768], P(('dp', 'feat'))
- updated_coef: float32 [128, 256], P(('dp', 'feat'))
- fixed_grad: float32 [2048, 512], P('feat')
Inputs may be any that keep to these rules, and one draw needn't show every extreme that they name: `row_slot`: each owner receives the same number of rows, 256, 128 or 64, from every device of its feat column; some owner receives 256 from every device. The rows one device sends to one owner take that owner's slots 0, 1, 2 and so on, each slot once. `tile_source`: every received row appears at exactly one position. An owner's members, in order, take consecutive runs of tiles; a member's rows fill its tiles from the first position on, and the rest of its last tile is padding, as are the tiles past all members. `member_tiles`: A member's tiles are its received rows divided by 128, rounded up; a device's members use at most 19 tiles in all, exactly 19 on the owners that receive 256 rows from every device.
All inputs are finite; a program needn't handle non-finite values. No bound on the sum of `labels` on one device may be relied on, other than what follows from the above.
Results may differ from a plain program's by a relative error of at most 0.0013.
Values may be sent and summed in bfloat16 or wider, within the bound.
No kernel may reach another device: no remote copies, remote signals or barrier semaphores. Data moves between devices by JAX's collectives and lax.ppermute only.
A program may use at most 64 MiB of HBM per device.

v0:
```python
import jax
import jax.numpy as jnp
from jax import lax
from jax.sharding import PartitionSpec as P

CG_ITERS = 2
TILE = 128
ridge_member = 1.0
ridge_fixed = 1.0
highest = lax.Precision.HIGHEST


def member_frame(tile_counts, tile_total, member_count):
    tile_ends = jnp.cumsum(tile_counts)
    positions = jnp.arange(tile_total, dtype=jnp.int32)
    member_index = jnp.sum((positions[:, None] >= tile_ends[None, :]).astype(jnp.int32), axis=1)
    return (member_index[:, None] == jnp.arange(member_count, dtype=jnp.int32)[None, :]).astype(
        jnp.float32
    )


def per_tile(tile_member, values):
    return jnp.dot(tile_member, values, precision=highest, preferred_element_type=jnp.float32)


def per_member(tile_member, values):
    return jnp.dot(tile_member.T, values, precision=highest, preferred_element_type=jnp.float32)


def row_dots(feats_wide, tile_vectors):
    return jnp.einsum("tri,ti->tr", feats_wide, tile_vectors, precision=highest)


def row_sums(row_weights, feats_wide):
    return jnp.einsum("tr,tri->ti", row_weights, feats_wide, precision=highest)


def body(
    member_feats,
    labels,
    fixed_values,
    fixed_blocks,
    fixed_coef,
    member_coef,
    row_slot,
    tile_source,
    member_tiles,
):
    dp_count = lax.axis_size("dp")
    rows_here = member_feats.shape[0]
    width = member_feats.shape[1]
    member_count = member_coef.shape[0]
    block_count = fixed_coef.shape[0]
    capacity = 2 * rows_here // dp_count
    slot_total = dp_count * capacity
    tile_total = tile_source.shape[0] // TILE
    block_index = fixed_blocks[:, 0]
    one_hot = (block_index[:, None] == jnp.arange(block_count, dtype=jnp.int32)[None, :]).astype(
        jnp.float32
    )
    looked_up = jnp.dot(one_hot, fixed_coef, precision=highest, preferred_element_type=jnp.float32)
    partial_value = jnp.sum(fixed_values.astype(jnp.float32) * looked_up, axis=1)
    fixed_score = lax.psum_scatter(partial_value, "feat", scatter_dimension=0, tiled=True)
    send_feats = jnp.zeros((slot_total, width), jnp.bfloat16).at[row_slot].set(member_feats)
    send_score = (
        jnp.zeros((slot_total,), jnp.bfloat16).at[row_slot].set(fixed_score.astype(jnp.bfloat16))
    )
    send_label = (
        jnp.zeros((slot_total,), jnp.bfloat16).at[row_slot].set(labels.astype(jnp.bfloat16))
    )
    got_feats, got_score, got_label = (
        lax.all_to_all(
            send_feats.reshape(dp_count, capacity, width),
            "dp",
            split_axis=0,
            concat_axis=0,
            tiled=True,
        ),
        lax.all_to_all(
            send_score.reshape(dp_count, capacity), "dp", split_axis=0, concat_axis=0, tiled=True
        ),
        lax.all_to_all(
            send_label.reshape(dp_count, capacity), "dp", split_axis=0, concat_axis=0, tiled=True
        ),
    )
    padded_feats = jnp.concatenate(
        [got_feats.reshape(slot_total, width), jnp.zeros((1, width), jnp.bfloat16)], axis=0
    )
    padded_score = jnp.concatenate(
        [got_score.reshape(slot_total), jnp.zeros((1,), jnp.bfloat16)], axis=0
    )
    padded_label = jnp.concatenate(
        [got_label.reshape(slot_total), jnp.zeros((1,), jnp.bfloat16)], axis=0
    )
    feats_wide = padded_feats[tile_source].astype(jnp.float32).reshape(tile_total, TILE, width)
    tile_fixed = padded_score[tile_source].astype(jnp.float32).reshape(tile_total, TILE)
    tile_label = padded_label[tile_source].astype(jnp.float32).reshape(tile_total, TILE)
    tile_member = member_frame(member_tiles, tile_total, member_count)
    logits = tile_fixed + row_dots(feats_wide, per_tile(tile_member, member_coef))
    probability = jax.nn.sigmoid(logits)
    weight = probability * (1.0 - probability)
    gradient = (
        per_member(tile_member, row_sums(tile_label - probability, feats_wide))
        - ridge_member * member_coef
    )
    diagonal = per_member(tile_member, row_sums(weight, feats_wide * feats_wide)) + ridge_member
    step_sum = jnp.zeros_like(member_coef)
    remain = gradient
    scaled = remain / diagonal
    search = scaled
    inner_product = jnp.sum(remain * scaled, axis=1)
    for iteration in range(CG_ITERS):
        projected = row_dots(feats_wide, per_tile(tile_member, search))
        image = (
            per_member(tile_member, row_sums(weight * projected, feats_wide))
            + ridge_member * search
        )
        alpha_step = inner_product / jnp.sum(search * image, axis=1)
        step_sum = step_sum + alpha_step[:, None] * search
        if iteration + 1 < CG_ITERS:
            remain = remain - alpha_step[:, None] * image
            scaled = remain / diagonal
            inner_next = jnp.sum(remain * scaled, axis=1)
            search = scaled + (inner_next / inner_product)[:, None] * search
            inner_product = inner_next
    updated_coef = member_coef + step_sum
    new_scores = row_dots(feats_wide, per_tile(tile_member, updated_coef)).reshape(-1)
    back_scores = (
        jnp.zeros((slot_total + 1,), jnp.float32).at[tile_source].set(new_scores)[:slot_total]
    )
    returned = lax.all_to_all(
        back_scores.reshape(dp_count, capacity), "dp", split_axis=0, concat_axis=0, tiled=True
    )
    member_score = returned.reshape(slot_total)[row_slot]
    margin = fixed_score + member_score
    residual = labels.astype(jnp.float32) - jax.nn.sigmoid(margin)
    group_residual = lax.all_gather(residual, "feat", axis=0, tiled=True)
    weighted_hot = one_hot * group_residual[:, None]
    contribution = jnp.dot(
        weighted_hot.T,
        fixed_values.astype(jnp.float32),
        precision=highest,
        preferred_element_type=jnp.float32,
    )
    summed = lax.psum(contribution, "dp")
    fixed_grad = ridge_fixed * fixed_coef - summed / dp_count
    return (margin, updated_coef, fixed_grad)


def solution(mesh):
    placed = (
        P(("dp", "feat"), None),
        P(("dp", "feat")),
        P("dp", "feat"),
        P("dp", "feat"),
        P("feat", None),
        P(("dp", "feat"), None),
        P(("dp", "feat")),
        P(("dp", "feat")),
        P(("dp", "feat")),
    )
    return jax.shard_map(
        body,
        mesh=mesh,
        in_specs=placed,
        out_specs=(P(("dp", "feat")), P(("dp", "feat"), None), P("feat", None)),
        check_vma=False,
    )
```

profile of v0, /device:TPU:0, one launch (start us, length us, event | category | flops | bytes accessed | tf_op | source)
XLA Modules:
  0.0 260.8 jit_solution(10872461917790779837)
XLA Ops:
  7.2 0.7 broadcast_clamp_fusion
  7.9 6.5 %copy.17 = bf16[4096,512]{0,1:T(8,128)(2,1)} copy(bf16[4096,512]{1,0:T(8,128)(2,1)} %param.11) | data formatting | bytes 8388608 | tf_op args[2]
  14.4 10.0 %multiply_reduce_fusion = f32[4096]{0:T(1024)S(1)} fusion(bf16[4096,512]{0,1:T(8,128)(2,1)} %copy.17, f32[512,512]{1,0:T(8,128)S(1)} %copy-done, s32[4096]{0:T(1024)S(1)} %bitcast.111), kind=kOutput, calls=%fused_computation.10 | convolution fusion | flops 12893286400 | bytes 5275648 | tf_op jit(solution)/shard_map/dot_general | solution.py:61
  24.4 12.7 %all-reduce.1 = f32[4096]{0:T(1024)S(1)} all-reduce(f32[4096]{0:T(1024)S(1)} %multiply_reduce_fusion), channel_id=2, replica_groups=mesh['dp'=8,'feat'=4] {'feat'}, use_global_device_ids=true, to_apply=%region_1.0.clone | all-reduce | flops 4096 | bytes 32768
  37.1 0.6 dynamic-slice
  38.4 7.6 %scatter_custom_fusion.2 = bf16[2048]{0:T(1024)(128)(2,1)S(1)} fusion(s32[1024]{0:T(1024)S(1)} %get-tuple-element.10, bf16[1024]{0:T(1024)(128)(2,1)S(1)} %dynamic-slice.4, bf16[]{:T(256)} %constant.11.clone.1), kind=kCustom, calls=%fused_computation.96 | custom fusion | bytes 4098 | tf_op jit(solution)/shard_map/scatter | solution.py:66
  46.0 0.5 broadcast.80
  46.5 0.7 reduce.2
  47.2 0.6 reshape.204
  47.8 5.8 %all-to-all-start.2 = ((bf16[8,2,128]{2,1,0:T(2,128)(2,1)}), bf16[8,2,128]{2,1,0:T(2,128)(2,1)S(1)}, u32[]{:S(2)}, u32[]{:S(2)}) async-start(bf16[8,2,128]{2,1,0:T(2,128)(2,1)} %reshape.204), calls=%async_computation.2 | async-start | bytes 8192 | tf_op jit(solution)/shard_map/all_to_all | solution.py:79
  53.6 7.6 %scatter_custom_fusion.1 = bf16[2048]{0:T(1024)(128)(2,1)S(1)} fusion(s32[1024]{0:T(1024)S(1)} %get-tuple-element.10, bf16[1024]{0:T(1024)(128)(2,1)S(1)} %convert_element_type.38, bf16[]{:T(256)} %constant.11.clone.1), kind=kCustom, calls=%fused_computation.98 | custom fusion | bytes 4098 | tf_op jit(solution)/shard_map/scatter | solution.py:69
  61.2 0.7 reduce.3
  61.9 0.6 reshape.202
  62.5 6.0 %all-to-all-start.1 = ((bf16[8,2,128]{2,1,0:T(2,128)(2,1)}), bf16[8,2,128]{2,1,0:T(2,128)(2,1)S(1)}, u32[]{:S(2)}, u32[]{:S(2)}) async-start(bf16[8,2,128]{2,1,0:T(2,128)(2,1)} %reshape.202), calls=%async_computation.1 | async-start | bytes 8192 | tf_op jit(solution)/shard_map/all_to_all | solution.py:82
  68.5 6.4 %scatter_custom_fusion = bf16[2048,256]{1,0:T(8,128)(2,1)} fusion(s32[1024]{0:T(1024)S(1)} %get-tuple-element.10, bf16[1024,256]{1,0:T(8,128)(2,1)} %param.9, bf16[]{:T(256)} %constant.11.clone.1), kind=kCustom, calls=%fused_computation.31 | custom fusion | bytes 1049088 | tf_op jit(solution)/shard_map/scatter | solution.py:64
  74.9 6.1 %all-to-all-start = ((bf16[8,256,256]{2,1,0:T(8,128)(2,1)}), bf16[8,256,256]{2,1,0:T(8,128)(2,1)S(1)}, u32[]{:S(2)}, u32[]{:S(2)}) async-start(bf16[8,256,256]{2,1,0:T(8,128)(2,1)} %bitcast.1), calls=%async_computation | async-start | bytes 2097152 | tf_op jit(solution)/shard_map/all_to_all | solution.py:72
  81.0 0.3 all-reduce.4.cloned.1.call-start
  81.3 0.2 reduce-window.8
  81.5 0.1 convert_reduce_fusion
  81.6 0.2 convolution_bitcast_fusion.3
  81.9 14.7 %gather_fusion.2 = bf16[2432]{0:T(1024)(128)(2,1)S(1)} fusion(bf16[2049]{0:T(1024)(128)(2,1)S(1)} %get-tuple-element.14, s32[3072]{0:T(1024)S(1)} %pad_clamp_fusion), kind=kCustom, calls=%fused_computation.2 | custom fusion | bytes 19456 | tf_op jit(solution)/shard_map/gather | solution.py:96
  96.6 14.7 %gather_fusion.1 = bf16[2432]{0:T(1024)(128)(2,1)S(1)} fusion(bf16[2049]{0:T(1024)(128)(2,1)S(1)} %get-tuple-element.15, s32[3072]{0:T(1024)S(1)} %pad_clamp_fusion), kind=kCustom, calls=%fused_computation.1 | custom fusion | bytes 19456 | tf_op jit(solution)/shard_map/gather | solution.py:97
  111.4 7.8 %gather_fusion = bf16[2432,256]{1,0:T(8,128)(2,1)S(1)} fusion(bf16[2049,256]{1,0:T(8,128)(2,1)S(1)} %concatenate.9, s32[3072]{0:T(1024)S(1)} %pad_clamp_fusion), kind=kCustom, calls=%fused_computation | custom fusion | bytes 2500096 | tf_op jit(solution)/shard_map/gather | solution.py:95
  119.2 1.1 fusion.28
  120.3 1.4 fusion.7
  121.7 0.3 convolution_add_fusion.2
  122.0 0.6 fusion.42
  122.6 0.3 fusion.61
  122.9 0.2 convolution_bitcast_fusion.2
  123.1 1.1 fusion.26
  124.2 0.6 fusion.39
  124.8 0.4 multiply_reduce_fusion.2
  125.2 0.2 multiply_reduce_fusion.1
  125.5 0.2 convolution_bitcast_fusion.1
  125.7 1.1 fusion.24
  126.8 0.6 fusion.37
  127.4 0.4 fusion.11
  127.8 0.1 add_add_fusion
  127.9 0.2 convolution_bitcast_fusion
  128.1 1.1 fusion.22
  129.2 12.4 %scatter_custom_fusion.3 = f32[2049]{0:T(1024)S(1)} fusion(s32[2432]{0:T(1024)S(1)} %compare_select_fusion, f32[2432]{0:T(1024)S(1)} %bitcast.110, f32[]{:T(128)} %constant.8.clone.1), kind=kCustom, calls=%fused_computation.84 | custom fusion | bytes 8200 | tf_op jit(solution)/shard_map/scatter | solution.py:129
  141.6 12.0 %all_to_all.34 = f32[8,1,256]{2,1,0:T(1,128)S(1)} all-to-all(f32[8,1,256]{2,1,0:T(1,128)S(1)} %bitcast.105), channel_id=1, replica_groups=mesh['dp'=8,'feat'=4] {'dp'}, dimensions={0} | all-to-all | bytes 16384 | tf_op jit(solution)/shard_map/all_to_all | solution.py:131
  153.6 6.1 %gather_fusion.3 = f32[1024]{0:T(1024)S(1)} fusion(f32[2048]{0:T(1024)S(1)} %bitcast.95, s32[1024]{0:T(1024)S(1)} %get-tuple-element.9), kind=kCustom, calls=%fused_computation.3 | custom fusion | bytes 12288 | tf_op jit(solution)/shard_map/gather | solution.py:134
  159.8 0.6 divide_subtract_fusion
  160.4 5.5 %all_gather.3 = f32[4096]{0:T(1024)S(1)} all-gather(f32[1024]{0:T(1024)S(1)} %get-tuple-element.5), channel_id=1, replica_groups=mesh['dp'=8,'feat'=4] {'feat'}, dimensions={0}, use_global_device_ids=true | all-gather | bytes 20480 | tf_op jit(solution)/shard_map/all_gather | solution.py:137
  165.8 11.0 %fusion = f32[512,512]{1,0:T(8,128)} fusion(bf16[4096,512]{1,0:T(8,128)(2,1)} %param.11, f32[4096]{0:T(1024)S(1)} %all_gather.3, s32[4096]{0:T(1024)S(1)} %bitcast.112), kind=kOutput, calls=%fused_computation.8 | convolution fusion | flops 12889096192 | bytes 5275648 | tf_op jit(solution)/shard_map/dot_general | solution.py:139
  176.9 74.7 %all-reduce.4.cloned.1.call-done = f32[512,512]{1,0:T(8,128)} async-done(((f32[512,512]{1,0:T(8,128)}), f32[512,512]{1,0:T(8,128)}) %all-reduce.4.cloned.1.call-update) | async-done | bytes 1048592 | tf_op jit(solution)/shard_map/psum | solution.py:145
  251.6 2.4 multiply_subtract_fusion
  (43 shorter events, 0.5 us)
Async XLA Ops:
  7.9 6.5 %copy-start = (f32[512,512]{1,0:T(8,128)S(1)}, f32[512,512]{1,0:T(8,128)}, u32[]{:S(2)}) copy-start(f32[512,512]{1,0:T(8,128)} %param.13) | copy-start | bytes 3145732
  7.9 6.5 %copy-start.5 = (s32[4096,1]{0,1:T(1,128)S(1)}, s32[4096,1]{0,1:T(1,128)}, u32[]{:S(2)}) copy-start(s32[4096,1]{0,1:T(1,128)} %param.12) | copy-start | bytes 49156
  14.4 22.7 %copy-start.7 = (u32[32]{0:T(128)S(1)}, u32[32]{0:T(128)}, u32[]{:S(2)}) copy-start(u32[32]{0:T(128)} %constant.35) | copy-start | bytes 388
  14.4 39.2 %copy-start.1 = (s32[1024]{0:T(1024)S(1)}, s32[1024]{0:T(1024)}, u32[]{:S(2)}) copy-start(s32[1024]{0:T(1024)} %param.10) | copy-start | bytes 12292
  47.8 14.7 %all-to-all-start.2 = ((bf16[8,2,128]{2,1,0:T(2,128)(2,1)}), bf16[8,2,128]{2,1,0:T(2,128)(2,1)S(1)}, u32[]{:S(2)}, u32[]{:S(2)}) async-start(bf16[8,2,128]{2,1,0:T(2,128)(2,1)} %reshape.204), calls=%async_computation.2 | async-start | bytes 8192 | tf_op jit(solution)/shard_map/all_to_all | solution.py:79
  62.5 12.4 %all-to-all-start.1 = ((bf16[8,2,128]{2,1,0:T(2,128)(2,1)}), bf16[8,2,128]{2,1,0:T(2,128)(2,1)S(1)}, u32[]{:S(2)}, u32[]{:S(2)}) async-start(bf16[8,2,128]{2,1,0:T(2,128)(2,1)} %reshape.202), calls=%async_computation.1 | async-start | bytes 8192 | tf_op jit(solution)/shard_map/all_to_all | solution.py:82
  74.9 6.4 %copy-start.6 = (s32[4]{0:T(128)S(1)}, s32[4]{0:T(128)}, u32[]{:S(2)}) copy-start(s32[4]{0:T(128)} %param.17) | copy-start | bytes 52
  74.9 6.6 %copy-start.2 = (s32[2432]{0:T(1024)S(1)}, s32[2432]{0:T(1024)}, u32[]{:S(2)}) copy-start(s32[2432]{0:T(1024)} %param.16) | copy-start | bytes 29188
  74.9 6.7 %copy-start.3 = (f32[4,256]{1,0:T(4,128)S(1)}, f32[4,256]{1,0:T(4,128)}, u32[]{:S(2)}) copy-start(f32[4,256]{1,0:T(4,128)} %param.14) | copy-start | bytes 12292
  74.9 36.5 %all-to-all-start = ((bf16[8,256,256]{2,1,0:T(8,128)(2,1)}), bf16[8,256,256]{2,1,0:T(8,128)(2,1)S(1)}, u32[]{:S(2)}, u32[]{:S(2)}) async-start(bf16[8,256,256]{2,1,0:T(8,128)(2,1)} %bitcast.1), calls=%async_computation | async-start | bytes 2097152 | tf_op jit(solution)/shard_map/all_to_all | solution.py:72
  81.0 170.6 %all-reduce.4.cloned.1.call-start = ((), (), s32[]{:S(2)}) async-start(), calls=%async_computation.4 | async-start | bytes 2097152 | tf_op jit(solution)/shard_map/psum | solution.py:145
  127.9 31.9 %copy-start.4 = (f32[4,256]{1,0:T(4,128)}, f32[4,256]{1,0:T(4,128)S(1)}, u32[]{:S(2)}) copy-start(f32[4,256]{1,0:T(4,128)S(1)} %add_add_fusion) | copy-start | bytes 12292
Sparse Core Ops, SparseCore 0:
  177.0 74.5 all-reduce.3
where the time goes:
time: 261 us
  local copies, waits for them, and re-layouts  86.3 us (33%)
  waiting for transfers between devices  74.7 us (29%)
  matrix products  30.6 us (12%)
  blocking collectives  30.2 us (12%)
  starting transfers between devices  18.2 us (7%)
  between operations  15 us (6%)
  other arithmetic  5.88 us (2%)
    psum x1, waiting for transfers between devices, body(): summed = lax.psum(contribution, 'dp')  74.7 us
    scatter x2, local copies, waits for them, and re-layouts, body(): jnp.zeros((slot_total,), jnp.bfloat16).at[row_slot]  15.2 us
    gather x1, local copies, waits for them, and re-layouts, body(): padded_score[tile_source].astype(jnp.float32).reshape(tile_total, TILE)  14.7 us
    gather x1, local copies, waits for them, and re-layouts, body(): padded_label[tile_source].astype(jnp.float32).reshape(tile_total, TILE)  14.7 us
    unnamed x1, blocking collectives  12.7 us
    scatter x1, local copies, waits for them, and re-layouts, body(): jnp.zeros((slot_total + 1,), jnp.float32).at[tile_source].set(new_scores)  12.4 us
    all_to_all x1, blocking collectives, body(): lax.all_to_all(back_scores.reshape(dp_count, capacity), 'dp', split_axis=...  12 us
    dot_general x1, matrix products, body(): jnp.dot(weighted_hot.T, fixed_values.astype(jnp.float32), precision=highe...  11 us
  transfers between devices with their start and end apart: 4, of which 1 were waited for; matrix products, arithmetic and copies ran while one was open for 17% of the time, Pallas kernels for 0%

commit v1 on v0

--- a/solution.py
+++ b/solution.py
@@ -142,7 +142,7 @@
         precision=highest,
         preferred_element_type=jnp.float32,
     )
-    summed = lax.psum(contribution, "dp")
+    summed = jnp.sum(lax.all_gather(contribution, "dp"), axis=0)
     fixed_grad = ridge_fixed * fixed_coef - summed / dp_count
     return (margin, updated_coef, fixed_grad)
 

time: 261 us -> 312 us (1.20)
  waiting for transfers between devices: 74.7 us -> 122 us
  other arithmetic: 5.88 us -> 9.85 us
    all_gather x0 -> x1, waiting for transfers between devices: none -> 122 us  [body(): summed = jnp.sum(lax.all_gather(contribution, 'dp'), axis=0)]
    psum x1 -> x0, waiting for transfers between devices: 74.7 us -> none  [body(): summed = lax.psum(contribution, 'dp')]
    reduce_sum x0 -> x1, other arithmetic: none -> 4.49 us  [body(): summed = jnp.sum(lax.all_gather(contribution, 'dp'), axis=0)]
  transfers between devices with their start and end apart: 4 -> 4, of which waited for: 1 -> 1; matrix products, arithmetic and copies ran while one was open for 17% -> 20% of each run, Pallas kernels for 0% -> 0%
where the time goes in v1:
time: 312 us; the launch traced here: 311 us
  waiting for transfers between devices  122 us (39%)
  local copies, waits for them, and re-layouts  86.2 us (28%)
  matrix products  30.7 us (10%)
  blocking collectives  28.2 us (9%)
  starting transfers between devices  19.4 us (6%)
  between operations  15 us (5%)
  other arithmetic  9.85 us (3%)
    all_gather x1, waiting for transfers between devices, body(): summed = jnp.sum(lax.all_gather(contribution, 'dp'), axis=0)  122 us
    scatter x2, local copies, waits for them, and re-layouts, body(): jnp.zeros((slot_total,), jnp.bfloat16).at[row_slot]  15.2 us
    gather x1, local copies, waits for them, and re-layouts, body(): padded_label[tile_source].astype(jnp.float32).reshape(tile_total, TILE)  14.7 us
    gather x1, local copies, waits for them, and re-layouts, body(): padded_score[tile_source].astype(jnp.float32).reshape(tile_total, TILE)  14.7 us
    scatter x1, local copies, waits for them, and re-layouts, body(): jnp.zeros((slot_total + 1,), jnp.float32).at[tile_source].set(new_scores)  12.4 us
    all_to_all x1, blocking collectives, body(): lax.all_to_all(back_scores.reshape(dp_count, capacity), 'dp', split_axis=...  12 us
    dot_general x1, matrix products, body(): jnp.dot(weighted_hot.T, fixed_values.astype(jnp.float32), precision=highe...  11 us
    unnamed x1, blocking collectives  10.7 us
  transfers between devices with their start and end apart: 4, of which 1 were waited for; matrix products, arithmetic and copies ran while one was open for 20% of the time, Pallas kernels for 0%

profile of v1, /device:TPU:0, one launch (start us, length us, event | category | flops | bytes accessed | tf_op | source)
XLA Modules:
  0.0 311.2 jit_solution(16000938620939031829)
XLA Ops:
  7.2 0.7 convert_element_type.38
  7.9 0.7 broadcast_clamp_fusion
  8.5 7.6 %scatter_custom_fusion.1 = bf16[2048]{0:T(1024)(128)(2,1)S(1)} fusion(s32[1024]{0:T(1024)S(1)} %get-tuple-element.10, bf16[1024]{0:T(1024)(128)(2,1)S(1)} %convert_element_type.38, bf16[]{:T(256)} %constant.11.clone.1), kind=kCustom, calls=%fused_computation.98 | custom fusion | bytes 4098 | tf_op jit(solution)/shard_map/scatter | solution.py:69
  16.2 0.5 broadcast.80
  16.7 0.7 reduce.3
  17.3 0.6 reshape.203
  17.9 7.3 %all-to-all-start.1 = ((bf16[8,2,128]{2,1,0:T(2,128)(2,1)}), bf16[8,2,128]{2,1,0:T(2,128)(2,1)S(1)}, u32[]{:S(2)}, u32[]{:S(2)}) async-start(bf16[8,2,128]{2,1,0:T(2,128)(2,1)} %reshape.203), calls=%async_computation.1 | async-start | bytes 8192 | tf_op jit(solution)/shard_map/all_to_all | solution.py:82
  25.2 6.5 %copy.17 = bf16[4096,512]{0,1:T(8,128)(2,1)} copy(bf16[4096,512]{1,0:T(8,128)(2,1)} %param.11) | data formatting | bytes 8388608 | tf_op args[2]
  31.8 10.1 %multiply_reduce_fusion = f32[4096]{0:T(1024)S(1)} fusion(bf16[4096,512]{0,1:T(8,128)(2,1)} %copy.17, f32[512,512]{1,0:T(8,128)S(1)} %copy-done, s32[4096]{0:T(1024)S(1)} %bitcast.117), kind=kOutput, calls=%fused_computation.10 | convolution fusion | flops 12893286400 | bytes 5275648 | tf_op jit(solution)/shard_map/dot_general | solution.py:61
  41.9 10.7 %all-reduce.1 = f32[4096]{0:T(1024)S(1)} all-reduce(f32[4096]{0:T(1024)S(1)} %multiply_reduce_fusion), channel_id=3, replica_groups=mesh['dp'=8,'feat'=4] {'feat'}, use_global_device_ids=true, to_apply=%region_1.0.clone | all-reduce | flops 4096 | bytes 32768
  52.5 0.6 dynamic-slice
  53.8 7.6 %scatter_custom_fusion.2 = bf16[2048]{0:T(1024)(128)(2,1)S(1)} fusion(s32[1024]{0:T(1024)S(1)} %get-tuple-element.10, bf16[1024]{0:T(1024)(128)(2,1)S(1)} %dynamic-slice.4, bf16[]{:T(256)} %constant.11.clone.1), kind=kCustom, calls=%fused_computation.96 | custom fusion | bytes 4098 | tf_op jit(solution)/shard_map/scatter | solution.py:66
  61.4 0.7 reduce.2
  62.1 0.6 reshape.205
  62.7 5.7 %all-to-all-start.2 = ((bf16[8,2,128]{2,1,0:T(2,128)(2,1)}), bf16[8,2,128]{2,1,0:T(2,128)(2,1)S(1)}, u32[]{:S(2)}, u32[]{:S(2)}) async-start(bf16[8,2,128]{2,1,0:T(2,128)(2,1)} %reshape.205), calls=%async_computation.2 | async-start | bytes 8192 | tf_op jit(solution)/shard_map/all_to_all | solution.py:79
  68.4 6.4 %scatter_custom_fusion = bf16[2048,256]{1,0:T(8,128)(2,1)} fusion(s32[1024]{0:T(1024)S(1)} %get-tuple-element.10, bf16[1024,256]{1,0:T(8,128)(2,1)} %param.9, bf16[]{:T(256)} %constant.11.clone.1), kind=kCustom, calls=%fused_computation.31 | custom fusion | bytes 1049088 | tf_op jit(solution)/shard_map/scatter | solution.py:64
  74.8 6.1 %all-to-all-start = ((bf16[8,256,256]{2,1,0:T(8,128)(2,1)}), bf16[8,256,256]{2,1,0:T(8,128)(2,1)S(1)}, u32[]{:S(2)}, u32[]{:S(2)}) async-start(bf16[8,256,256]{2,1,0:T(8,128)(2,1)} %bitcast.1), calls=%async_computation | async-start | bytes 2097152 | tf_op jit(solution)/shard_map/all_to_all | solution.py:72
  80.9 0.3 all-gather.3.cloned.1.call-start
  81.2 0.2 reduce-window.8
  81.5 0.2 convolution_bitcast_fusion.3
  81.8 14.7 %gather_fusion.2 = bf16[2432]{0:T(1024)(128)(2,1)S(1)} fusion(bf16[2049]{0:T(1024)(128)(2,1)S(1)} %get-tuple-element.14, s32[3072]{0:T(1024)S(1)} %pad_clamp_fusion), kind=kCustom, calls=%fused_computation.2 | custom fusion | bytes 19456 | tf_op jit(solution)/shard_map/gather | solution.py:96
  96.5 14.7 %gather_fusion.1 = bf16[2432]{0:T(1024)(128)(2,1)S(1)} fusion(bf16[2049]{0:T(1024)(128)(2,1)S(1)} %get-tuple-element.15, s32[3072]{0:T(1024)S(1)} %pad_clamp_fusion), kind=kCustom, calls=%fused_computation.1 | custom fusion | bytes 19456 | tf_op jit(solution)/shard_map/gather | solution.py:97
  111.3 7.8 %gather_fusion = bf16[2432,256]{1,0:T(8,128)(2,1)S(1)} fusion(bf16[2049,256]{1,0:T(8,128)(2,1)S(1)} %concatenate.9, s32[3072]{0:T(1024)S(1)} %pad_clamp_fusion), kind=kCustom, calls=%fused_computation | custom fusion | bytes 2500096 | tf_op jit(solution)/shard_map/gather | solution.py:95
  119.1 1.1 fusion.28
  120.2 1.4 fusion.7
  121.7 0.3 convolution_add_fusion.2
  121.9 0.6 fusion.42
  122.5 0.3 fusion.61
  122.8 0.2 convolution_bitcast_fusion.2
  123.0 1.1 fusion.26
  124.1 0.6 fusion.39
  124.7 0.4 multiply_reduce_fusion.2
  125.1 0.2 multiply_reduce_fusion.1
  125.4 0.2 convolution_bitcast_fusion.1
  125.6 1.1 fusion.24
  126.8 0.6 fusion.37
  127.4 0.4 fusion.11
  127.8 0.2 convolution_bitcast_fusion
  128.0 1.1 fusion.22
  129.1 12.4 %scatter_custom_fusion.3 = f32[2049]{0:T(1024)S(1)} fusion(s32[2432]{0:T(1024)S(1)} %compare_select_fusion, f32[2432]{0:T(1024)S(1)} %bitcast.116, f32[]{:T(128)} %constant.8.clone.1), kind=kCustom, calls=%fused_computation.84 | custom fusion | bytes 8200 | tf_op jit(solution)/shard_map/scatter | solution.py:129
  141.5 12.0 %all_to_all.34 = f32[8,1,256]{2,1,0:T(1,128)S(1)} all-to-all(f32[8,1,256]{2,1,0:T(1,128)S(1)} %bitcast.111), channel_id=1, replica_groups=mesh['dp'=8,'feat'=4] {'dp'}, dimensions={0} | all-to-all | bytes 16384 | tf_op jit(solution)/shard_map/all_to_all | solution.py:131
  153.5 6.1 %gather_fusion.3 = f32[1024]{0:T(1024)S(1)} fusion(f32[2048]{0:T(1024)S(1)} %bitcast.100, s32[1024]{0:T(1024)S(1)} %get-tuple-element.9), kind=kCustom, calls=%fused_computation.3 | custom fusion | bytes 12288 | tf_op jit(solution)/shard_map/gather | solution.py:134
  159.7 0.6 divide_subtract_fusion
  160.3 5.5 %all_gather.9 = f32[4096]{0:T(1024)S(1)} all-gather(f32[1024]{0:T(1024)S(1)} %get-tuple-element.5), channel_id=1, replica_groups=mesh['dp'=8,'feat'=4] {'feat'}, dimensions={0}, use_global_device_ids=true | all-gather | bytes 20480 | tf_op jit(solution)/shard_map/all_gather | solution.py:137
  165.8 11.0 %fusion = f32[512,512]{1,0:T(8,128)} fusion(bf16[4096,512]{1,0:T(8,128)(2,1)} %param.11, f32[4096]{0:T(1024)S(1)} %all_gather.9, s32[4096]{0:T(1024)S(1)} %bitcast.118), kind=kOutput, calls=%fused_computation.8 | convolution fusion | flops 12889096192 | bytes 5275648 | tf_op jit(solution)/shard_map/dot_general | solution.py:139
  176.8 121.8 %all-gather.3.cloned.1.call-done = f32[4096,512]{1,0:T(8,128)} async-done(((f32[512,512]{1,0:T(8,128)}), f32[4096,512]{1,0:T(8,128)}) %all-gather.3.cloned.1.call-update) | async-done | bytes 8388624 | tf_op jit(solution)/shard_map/all_gather | solution.py:145
  298.6 4.5 %reduce_sum.69 = f32[512,512]{1,0:T(8,128)S(1)} reduce(f32[8,512,512]{2,1,0:T(8,128)} %bitcast.109, f32[]{:T(128)} %constant.8.clone.1), dimensions={0}, to_apply=%region_12.13 | reduce | flops 1835008 | bytes 9437188 | tf_op jit(solution)/shard_map/reduce_sum | solution.py:145
  303.1 1.2 multiply_subtract_fusion
  (44 shorter events, 0.7 us)
Async XLA Ops:
  17.9 44.7 %all-to-all-start.1 = ((bf16[8,2,128]{2,1,0:T(2,128)(2,1)}), bf16[8,2,128]{2,1,0:T(2,128)(2,1)S(1)}, u32[]{:S(2)}, u32[]{:S(2)}) async-start(bf16[8,2,128]{2,1,0:T(2,128)(2,1)} %reshape.203), calls=%async_computation.1 | async-start | bytes 8192 | tf_op jit(solution)/shard_map/all_to_all | solution.py:82
  25.2 6.5 %copy-start = (f32[512,512]{1,0:T(8,128)S(1)}, f32[512,512]{1,0:T(8,128)}, u32[]{:S(2)}) copy-start(f32[512,512]{1,0:T(8,128)} %param.13) | copy-start | bytes 3145732
  25.2 6.5 %copy-start.5 = (s32[4096,1]{0,1:T(1,128)S(1)}, s32[4096,1]{0,1:T(1,128)}, u32[]{:S(2)}) copy-start(s32[4096,1]{0,1:T(1,128)} %param.12) | copy-start | bytes 49156
  31.8 20.8 %copy-start.7 = (u32[32]{0:T(128)S(1)}, u32[32]{0:T(128)}, u32[]{:S(2)}) copy-start(u32[32]{0:T(128)} %constant.35) | copy-start | bytes 388
  62.7 12.1 %all-to-all-start.2 = ((bf16[8,2,128]{2,1,0:T(2,128)(2,1)}), bf16[8,2,128]{2,1,0:T(2,128)(2,1)S(1)}, u32[]{:S(2)}, u32[]{:S(2)}) async-start(bf16[8,2,128]{2,1,0:T(2,128)(2,1)} %reshape.205), calls=%async_computation.2 | async-start | bytes 8192 | tf_op jit(solution)/shard_map/all_to_all | solution.py:79
  74.8 6.4 %copy-start.6 = (s32[4]{0:T(128)S(1)}, s32[4]{0:T(128)}, u32[]{:S(2)}) copy-start(s32[4]{0:T(128)} %param.17) | copy-start | bytes 52
  74.8 6.6 %copy-start.2 = (s32[2432]{0:T(1024)S(1)}, s32[2432]{0:T(1024)}, u32[]{:S(2)}) copy-start(s32[2432]{0:T(1024)} %param.16) | copy-start | bytes 29188
  74.8 6.7 %copy-start.3 = (f32[4,256]{1,0:T(4,128)S(1)}, f32[4,256]{1,0:T(4,128)}, u32[]{:S(2)}) copy-start(f32[4,256]{1,0:T(4,128)} %param.14) | copy-start | bytes 12292
  74.8 36.5 %all-to-all-start = ((bf16[8,256,256]{2,1,0:T(8,128)(2,1)}), bf16[8,256,256]{2,1,0:T(8,128)(2,1)S(1)}, u32[]{:S(2)}, u32[]{:S(2)}) async-start(bf16[8,256,256]{2,1,0:T(8,128)(2,1)} %bitcast.1), calls=%async_computation | async-start | bytes 2097152 | tf_op jit(solution)/shard_map/all_to_all | solution.py:72
  80.9 217.7 %all-gather.3.cloned.1.call-start = ((), (), s32[]{:S(2)}) async-start(), calls=%async_computation.4 | async-start | bytes 9437184 | tf_op jit(solution)/shard_map/all_gather | solution.py:145
  127.8 31.9 %copy-start.4 = (f32[4,256]{1,0:T(4,128)}, f32[4,256]{1,0:T(4,128)S(1)}, u32[]{:S(2)}) copy-start(f32[4,256]{1,0:T(4,128)S(1)} %add_add_fusion) | copy-start | bytes 12292
  153.5 6.2 %copy-start.1 = (s32[1024]{0:T(1024)S(1)}, s32[1024]{0:T(1024)}, u32[]{:S(2)}) copy-start(s32[1024]{0:T(1024)} %param.10) | copy-start | bytes 12292
Sparse Core Ops, SparseCore 0:
  176.9 121.6 all-gather.2
